TPU v7x, 1024 devices: a whole 4x4x32 slice. The times are simulated.
1024 devices in a mesh: dp: 32 (over x, z_lo), space: 8 (over z_hi, core), tm: 4 (over y).
Axes of the slice: x: 4, y: 4, z: 32 (z_hi: 4, z_lo: 8; z = z_hi * 8 + z_lo), core: 2. Of those that a mesh axis runs over, the one named last changes fastest.
Arguments:
- inputs: bfloat16 [32, 20, 128, 1024], P('dp', None, 'space', 'tm'), may hold values from -6 to 6
- out_grad: bfloat16 [32, 20, 128, 1024], P('dp', None, 'space', 'tm'), may hold values from -6 to 6
- norm_gain: float32 [1024], replicated, may hold values from 0.1 to 1.9
- pos_bias: float32 [16, 39], P('tm'), may hold values from -4 to 4
- w_query: bfloat16 [1024, 1024], P(None, 'tm'), may hold values from -0.1875 to 0.1875
- w_key: bfloat16 [1024, 1024], P(None, 'tm'), may hold values from -0.1875 to 0.1875
- w_value: bfloat16 [1024, 1024], P(None, 'tm'), may hold values from -0.1875 to 0.1875
- w_out: bfloat16 [1024, 1024], P('tm'), may hold values from -0.1875 to 0.1875
Outputs:
- block_out: bfloat16 [32, 20, 128, 1024], P('dp', None, 'space', 'tm')
- input_grad: bfloat16 [32, 20, 128, 1024], P('dp', None, 'space', 'tm')
- gain_grad: float32 [1024], P('tm')
- bias_grad: float32 [16, 39], P('tm')
All inputs are finite; a program needn't handle non-finite values.
Results may differ from a plain program's by a relative error of at most 0.0099.
Values may be sent and summed in bfloat16 or wider, within the bound.
A program may use at most 32 MiB of HBM per device.

v0:
```python
import jax
import jax.numpy as jnp
from jax import lax
from jax.sharding import PartitionSpec as P


def offset_table(frames):
    query_idx = lax.iota(jnp.int32, frames)
    key_idx = lax.iota(jnp.int32, frames)
    offsets = key_idx[None, :] - query_idx[:, None] + frames - 1
    columns = lax.iota(jnp.int32, 2 * frames - 1)
    return (offsets[:, :, None] == columns[None, None, :]).astype(jnp.float32)


def bias_rows(bias, table):
    return jnp.einsum("ho,qko->hqk", bias, table, precision=lax.Precision.HIGHEST)


def bias_back(score_sum, table):
    return jnp.einsum("hqk,qko->ho", score_sum, table, precision=lax.Precision.HIGHEST)


def soft_probs(queries, key_rows, rel_bias, scale):
    scores = jnp.einsum("bqphd,bkphd->bphqk", queries, key_rows, preferred_element_type=jnp.float32)
    scores = scores * scale + rel_bias[None, None]
    log_total = jax.nn.logsumexp(scores, axis=-1, keepdims=True)
    return jnp.exp(scores - log_total).astype(jnp.bfloat16)


def attend(probs, value_rows):
    return jnp.einsum(
        "bphqk,bkphd->bqphd", probs, value_rows, preferred_element_type=jnp.float32
    ).astype(jnp.bfloat16)


def score_grads(probs, grad_att, value_rows, scale):
    grad_prob = jnp.einsum(
        "bqphd,bkphd->bphqk", grad_att, value_rows, preferred_element_type=jnp.float32
    )
    probs_full = probs.astype(jnp.float32)
    row_dot = jnp.sum(probs_full * grad_prob, axis=-1, keepdims=True)
    grad_score = probs_full * (grad_prob - row_dot)
    return (grad_score, (grad_score * scale).astype(jnp.bfloat16))


def contract_keys(grad_scaled, key_rows):
    return jnp.einsum(
        "bphqk,bkphd->bqphd", grad_scaled, key_rows, preferred_element_type=jnp.float32
    ).astype(jnp.bfloat16)


def contract_queries(weights, rows):
    return jnp.einsum(
        "bphqk,bqphd->bkphd", weights, rows, preferred_element_type=jnp.float32
    ).astype(jnp.bfloat16)


def per_device(inputs, out_grad, norm_gain, pos_bias, w_query, w_key, w_value, w_out):
    clips, frames, pixels, width = inputs.shape
    group = pos_bias.shape[0]
    tm_count = lax.axis_size("tm")
    chans = width * tm_count
    head_dim = width // group
    scale = head_dim ** (-0.5)
    col_start = lax.axis_index("tm") * width
    x_local = inputs.astype(jnp.float32)
    x_whole = lax.all_gather(inputs, "tm", axis=3, tiled=True).astype(jnp.float32)
    scale_inv = lax.rsqrt(jnp.mean(x_whole * x_whole, axis=-1, keepdims=True) + 1e-06)
    normed = (x_whole * scale_inv * norm_gain).astype(jnp.bfloat16)

    def project(weight):
        out = jnp.einsum("bfpc,cd->bfpd", normed, weight, preferred_element_type=jnp.float32)
        return out.astype(jnp.bfloat16).reshape(clips, frames, pixels, group, head_dim)

    queries = project(w_query)
    key_rows = project(w_key)
    value_rows = project(w_value)
    table = offset_table(frames)
    probs = soft_probs(queries, key_rows, bias_rows(pos_bias, table), scale)
    attended = attend(probs, value_rows).reshape(clips, frames, pixels, width)
    partial_mix = jnp.einsum("bfpd,dc->bfpc", attended, w_out, preferred_element_type=jnp.float32)
    mixed = lax.psum_scatter(partial_mix, "tm", scatter_dimension=3, tiled=True)
    block_out = (x_local + mixed).astype(jnp.bfloat16)
    grad_att = jnp.einsum(
        "bfpc,dc->bfpd",
        lax.all_gather(out_grad, "tm", axis=3, tiled=True),
        w_out,
        preferred_element_type=jnp.float32,
    )
    grad_att = grad_att.astype(jnp.bfloat16).reshape(clips, frames, pixels, group, head_dim)
    grad_score, grad_scaled = score_grads(probs, grad_att, value_rows, scale)
    grad_query = contract_keys(grad_scaled, key_rows).reshape(clips, frames, pixels, width)
    grad_key = contract_queries(grad_scaled, queries).reshape(clips, frames, pixels, width)
    grad_value = contract_queries(probs, grad_att).reshape(clips, frames, pixels, width)
    gain_local = lax.dynamic_slice_in_dim(norm_gain, col_start, width, 0)

    def back_project(grads, weight):
        return jnp.einsum("bfpd,cd->bfpc", grads, weight, preferred_element_type=jnp.float32)

    partial_grad = (
        back_project(grad_query, w_query)
        + back_project(grad_key, w_key)
        + back_project(grad_value, w_value)
    )
    partial_inner = jnp.sum(partial_grad * norm_gain * x_whole, axis=-1, keepdims=True) / chans
    inner_copies = jnp.broadcast_to(partial_inner, (clips, frames, pixels, tm_count))
    grad_normed, inner = (
        lax.psum_scatter(partial_grad, "tm", scatter_dimension=3, tiled=True),
        lax.psum_scatter(inner_copies, "tm", scatter_dimension=3, tiled=True),
    )
    scale_grad = grad_normed * gain_local
    gain_part = jnp.sum(grad_normed * x_local * scale_inv, axis=(0, 1, 2))
    input_grad = (
        out_grad.astype(jnp.float32) + scale_inv * scale_grad - x_local * scale_inv**3 * inner
    )
    bias_part = bias_back(jnp.sum(grad_score, axis=(0, 1)), table)
    gain_grad, bias_grad = lax.psum((gain_part, bias_part), ("dp", "space"))
    return (block_out, input_grad.astype(jnp.bfloat16), gain_grad, bias_grad)


def solution(mesh):
    return jax.shard_map(
        per_device,
        mesh=mesh,
        in_specs=(
            P("dp", None, "space", "tm"),
            P("dp", None, "space", "tm"),
            P(),
            P("tm", None),
            P(None, "tm"),
            P(None, "tm"),
            P(None, "tm"),
            P("tm", None),
        ),
        out_specs=(
            P("dp", None, "space", "tm"),
            P("dp", None, "space", "tm"),
            P("tm"),
            P("tm", None),
        ),
        check_vma=False,
    )
```

profile of v0, /device:TPU:130, one launch (start us, length us, event | category | flops | bytes accessed | tf_op | source)
XLA Modules:
  0.0 1181.0 jit_solution(9918717991425233243)
XLA Ops:
  7.3 0.1 iota_compare_fusion
  7.4 1.4 convolution_bitcast_fusion.1
  8.9 0.1 copy.43
  9.0 13.8 %all_gather.6 = bf16[1,20,16,1024]{3,2,1,0:T(8,128)(2,1)S(1)} all-gather(bf16[1,20,16,256]{3,2,1,0:T(8,128)(2,1)} %param.8), channel_id=1, replica_groups=mesh['dp'=32,'space'=8,'tm'=4] {'tm'}, dimensions={3}, use_global_device_ids=true | all-gather | bytes 819200 | tf_op jit(solution)/shard_map/all_gather | solution.py:67
  22.7 0.2 fusion.1
  23.0 0.4 convolution_convert_fusion.6
  23.4 0.2 reshape.213
  23.6 0.4 copy-done.9
  24.0 0.4 convolution_convert_fusion.5
  24.4 0.2 reshape.214
  24.7 0.4 convolution_convert_fusion.7
  25.1 0.2 reshape.212
  25.3 0.3 copy-done.6
  25.5 13.5 %all_gather.7 = bf16[1,20,16,1024]{3,2,1,0:T(8,128)(2,1)S(1)} all-gather(bf16[1,20,16,256]{3,2,1,0:T(8,128)(2,1)S(1)} %copy-done.6), channel_id=1, replica_groups=mesh['dp'=32,'space'=8,'tm'=4] {'tm'}, dimensions={3}, use_global_device_ids=true | all-gather | bytes 819200 | tf_op jit(solution)/shard_map/all_gather | solution.py:86
  39.1 0.4 convolution_convert_fusion.4
  39.4 0.2 reshape.217
  39.6 0.7 fusion.47
  40.3 0.2 exponential_reduce_fusion
  40.6 0.1 exponential_convert_fusion
  40.7 0.4 fusion.11
  41.1 0.6 fusion.25
  41.7 2.6 fusion.48
  44.3 1.1 fusion.10
  45.4 1.2 fusion.9
  46.6 0.2 copy.55
  46.8 0.9 reshape.220
  47.7 0.2 copy.51
  47.8 0.9 reshape.218
  48.7 0.2 copy.53
  48.9 0.2 reshape.219
  49.2 0.5 copy-done.8
  49.7 1.5 fusion.19
  51.2 0.4 convolution_add_fusion.1
  51.5 0.5 copy-done.4
  52.1 1.5 fusion.4
  53.6 0.6 broadcast_in_dim.5
  54.3 0.7 reduce-scatter.6.cloned.1.call-update
  55.1 0.4 fusion.8
  55.5 0.2 copy.46
  55.7 0.2 reshape.215
  56.0 1.4 convolution_bitcast_fusion
  57.5 0.3 convolution_bitcast_fusion.2
  57.8 41.1 %reduce-scatter.8.cloned.1.call-done = f32[1,20,16,1]{1,2,0,3:T(8,128)} async-done(((f32[1,20,16,4]{1,2,0,3:T(8,128)}), f32[1,20,16,1]{1,2,0,3:T(8,128)}) %reduce-scatter.8.cloned.1.call-update) | async-done | bytes 1296 | tf_op jit(solution)/shard_map/reduce_scatter | solution.py:109
  98.9 0.8 copy.57
  99.7 45.4 %reduce-scatter.6.cloned.1.call-done = f32[1,20,16,256]{3,2,1,0:T(8,128)} async-done(((f32[1,20,16,1024]{3,2,1,0:T(8,128)}), f32[1,20,16,256]{3,2,1,0:T(8,128)}) %reduce-scatter.6.cloned.1.call-update) | async-done | bytes 327696 | tf_op jit(solution)/shard_map/reduce_scatter | solution.py:108
  145.1 46.2 %reduce-scatter.4.cloned.1.call-done = f32[1,20,16,256]{3,2,1,0:T(8,128)} async-done(((f32[1,20,16,1024]{3,2,1,0:T(8,128)}), f32[1,20,16,256]{3,2,1,0:T(8,128)}) %reduce-scatter.4.cloned.1.call-update) | async-done | bytes 327696 | tf_op jit(solution)/shard_map/reduce_scatter | solution.py:82
  191.2 2.0 fusion.41
  193.2 981.3 %all-reduce = (f32[256]{0:T(256)}, f32[4,39]{1,0:T(4,128)}) all-reduce(f32[256]{0:T(256)S(1)} %get-tuple-element.6, f32[4,39]{1,0:T(4,128)S(1)} %convolution_bitcast_fusion.2), channel_id=1, replica_groups=mesh['dp'=32,'space'=8,'tm'=4] {'dp','space'}, use_global_device_ids=true, to_apply=%region_9.0 | all-reduce | flops 412 | bytes 3296 | tf_op jit(solution)/shard_map/psum | solution.py:117
  (44 shorter events, 0.4 us)
Async XLA Ops:
  7.2 17.5 %copy-start = (bf16[1024,256]{1,0:T(8,128)(2,1)S(1)}, bf16[1024,256]{1,0:T(8,128)(2,1)}, u32[]{:S(2)}) copy-start(bf16[1024,256]{1,0:T(8,128)(2,1)} %param.14) | copy-start | bytes 1572868
  7.2 15.8 %copy-start.17 = (f32[1024]{0:T(1024)S(1)}, f32[1024]{0:T(1024)}, u32[]{:S(2)}) copy-start(f32[1024]{0:T(1024)} %param.10) | copy-start | bytes 12292
  7.2 15.8 %copy-start.11 = (bf16[1024,256]{1,0:T(8,128)(2,1)S(1)}, bf16[1024,256]{1,0:T(8,128)(2,1)}, u32[]{:S(2)}) copy-start(bf16[1024,256]{1,0:T(8,128)(2,1)} %param.12) | copy-start | bytes 1572868
  7.2 91.7 %reduce-scatter.8.cloned.1.call-start = ((), (), s32[]{:S(2)}) async-start(), calls=%async_computation.5 | async-start | bytes 40960 | tf_op jit(solution)/shard_map/reduce_scatter | solution.py:109
  7.3 15.5 %copy-start.14 = (s32[20,20]{0,1:T(8,128)}, s32[20,20]{0,1:T(8,128)S(1)}, u32[]{:S(2)}) copy-start(s32[20,20]{0,1:T(8,128)S(1)} %subtract_add_fusion) | copy-start | bytes 4804
  22.9 1.1 copy-start.9
  23.0 1.6 copy-start.12
  24.6 0.9 copy-start.6
  24.6 14.4 %copy-start.1 = (bf16[256,1024]{1,0:T(8,128)(2,1)S(1)}, bf16[256,1024]{1,0:T(8,128)(2,1)}, u32[]{:S(2)}) copy-start(bf16[256,1024]{1,0:T(8,128)(2,1)} %param.15) | copy-start | bytes 1572868
  46.6 1.1 copy-start.3
  46.6 2.2 copy-start.2
  48.7 0.9 copy-start.8
  49.7 1.5 copy-start.10
  51.1 0.9 copy-start.4
  54.3 90.8 %reduce-scatter.6.cloned.1.call-start = ((), (), s32[]{:S(2)}) async-start(), calls=%async_computation.4 | async-start | bytes 1638400 | tf_op jit(solution)/shard_map/reduce_scatter | solution.py:108
  55.0 136.2 %reduce-scatter.4.cloned.1.call-start = ((), (), s32[]{:S(2)}) async-start(), calls=%async_computation.3 | async-start | bytes 1638400 | tf_op jit(solution)/shard_map/reduce_scatter | solution.py:82
  55.9 1.6 copy-start.15
  55.9 1.6 copy-start.16
  55.9 135.3 %copy-start.5 = (bf16[1,20,16,256]{3,2,1,0:T(8,128)(2,1)S(1)}, bf16[1,20,16,256]{3,2,1,0:T(8,128)(2,1)}, u32[]{:S(2)}) copy-start(bf16[1,20,16,256]{3,2,1,0:T(8,128)(2,1)} %param.8) | copy-start | bytes 491524
  55.9 135.3 %copy-start.7 = (bf16[1,20,16,256]{3,2,1,0:T(8,128)(2,1)S(1)}, bf16[1,20,16,256]{3,2,1,0:T(8,128)(2,1)}, u32[]{:S(2)}) copy-start(bf16[1,20,16,256]{3,2,1,0:T(8,128)(2,1)} %param.9) | copy-start | bytes 491524
  56.0 135.3 %copy-start.13 = (f32[20,16]{1,0:T(8,128)S(1)}, f32[20,16]{1,0:T(8,128)}, u32[]{:S(2)}) copy-start(f32[20,16]{1,0:T(8,128)} %copy-done.12) | copy-start | bytes 3844
Sparse Core Ops, SparseCore 0:
  54.4 44.4 reduce-scatter.7
  102.7 42.2 reduce-scatter.5
  148.9 42.2 reduce-scatter.3
where the time goes:
time: 1180 us
  blocking collectives  1010 us (86%)
  waiting for transfers between devices  133 us (11%)
  between operations  14.1 us (1%)
  matrix products  12.3 us (1%)
    psum x1, blocking collectives, per_device(): gain_grad, bias_grad = lax.psum((gain_part, bias_part), ('dp', 'space'))  981 us
    reduce_scatter x1, waiting for transfers between devices, per_device(): mixed = lax.psum_scatter(partial_mix, 'tm', scatter_dimension=3, tiled=True)  46.2 us
    reduce_scatter x1, waiting for transfers between devices, per_device(): lax.psum_scatter(partial_grad, 'tm', scatter_dimension=3, tiled=True)  45.4 us
    reduce_scatter x1, waiting for transfers between devices, per_device(): lax.psum_scatter(inner_copies, 'tm', scatter_dimension=3, tiled=True)  41.1 us
  transfers between devices with their start and end apart: 3, of which 3 were waited for; matrix products, arithmetic and copies ran while one was open for 0% of the time, Pallas kernels for 0%

commit v1 on v0

v1 whole, which is shorter than its diff:
```python
import functools

import jax
import jax.numpy as jnp
from jax import lax
from jax.experimental import pallas as pl
from jax.experimental.pallas import tpu as pltpu
from jax.sharding import PartitionSpec as P

F32 = jnp.float32
BF16 = jnp.bfloat16
I32 = jnp.int32
NEG = -1e30
LANES = 128


def nn(a, b, precision=None):
    return lax.dot_general(
        a, b, (((1,), (0,)), ((), ())), precision=precision, preferred_element_type=F32
    )


def nt(a, b, precision=None):
    return lax.dot_general(
        a, b, (((1,), (1,)), ((), ())), precision=precision, preferred_element_type=F32
    )


def iota(shape, dim):
    return lax.broadcasted_iota(I32, shape, dim)


def onehot_rows(rows, cols, per):
    return (lax.div(iota((rows, cols), 0), per) == iota((rows, cols), 1)).astype(F32)


def onehot_cols(rows, cols, per):
    return (lax.div(iota((rows, cols), 1), per) == iota((rows, cols), 0)).astype(F32)


def kernel(
    cfg,
    x_hbm,
    g_hbm,
    gain_hbm,
    bias_hbm,
    wq_hbm,
    wk_hbm,
    wv_hbm,
    wo_hbm,
    bo_hbm,
    ig_hbm,
    gg_ref,
    bb_ref,
    x_all,
    g_all,
    w_all,
    wo,
    gain,
    bias,
    bm,
    probs,
    xg,
    qm,
    km,
    vm,
    gam,
    ks,
    vs,
    q_t,
    ga_t,
    sinv,
    att,
    gq_acc,
    gk_t,
    gv_t,
    gcat,
    gsum,
    mix_own,
    mix_send,
    mix_recv,
    ig_own,
    ig_send,
    ig_recv,
    p0_send,
    p0_recv,
    pay1,
    near_recv,
    pay2,
    far_recv,
    bo_st,
    ig_st,
    lsem,
    xsend,
    xrecv,
    gsend,
    grecv,
    msend,
    mrecv,
    isend,
    irecv,
    p0s,
    p0r,
    nsend,
    nrecv,
    fsend,
    frecv,
):
    frames, pixels, heads, n, xs, zl, zh, cores = cfg
    rows, width = x_hbm.shape
    chans = width * n
    head_dim = width // heads
    scale = head_dim ** (-0.5)
    me = lax.axis_index("tm")
    dp = lax.axis_index("dp")
    sp = lax.axis_index("space")
    my_x, my_zl = lax.div(dp, zl), lax.rem(dp, zl)
    my_zh, my_core = lax.div(sp, cores), lax.rem(sp, cores)

    ring = [(dp, sp, lax.rem(me + a, n)) for a in range(n)]
    shard = [lax.rem(me + a, n) for a in range(n)]
    near = [
        (my_x * zl + lax.rem(my_zl + b, zl), my_zh * cores + lax.rem(my_core + d, cores), me)
        for b in range(zl)
        for d in range(cores)
        if b or d
    ]
    far = [
        (lax.rem(my_x + b, xs) * zl + my_zl, lax.rem(my_zh + d, zh) * cores + my_core, me)
        for b in range(xs)
        for d in range(zh)
        if b or d
    ]

    def send(src, dst, ssem, rsem, to):
        return pltpu.make_async_remote_copy(
            src_ref=src,
            dst_ref=dst,
            send_sem=ssem,
            recv_sem=rsem,
            device_id=to,
            device_id_type=pl.DeviceIdType.MESH,
        )

    def cols(a):
        return pl.ds(pl.multiple_of(shard[a] * width, width), width)

    loads = [
        pltpu.make_async_copy(x_hbm, x_all.at[me], lsem.at[0]),
        pltpu.make_async_copy(gain_hbm, gain, lsem.at[1]),
        pltpu.make_async_copy(bias_hbm, bias, lsem.at[2]),
        pltpu.make_async_copy(wq_hbm, w_all.at[:, pl.ds(0, width)], lsem.at[3]),
        pltpu.make_async_copy(wk_hbm, w_all.at[:, pl.ds(width, width)], lsem.at[4]),
        pltpu.make_async_copy(wv_hbm, w_all.at[:, pl.ds(2 * width, width)], lsem.at[5]),
        pltpu.make_async_copy(wo_hbm, wo, lsem.at[6]),
        pltpu.make_async_copy(g_hbm, g_all.at[me], lsem.at[7]),
    ]
    for load in loads:
        load.start()

    barrier = pltpu.get_barrier_semaphore()
    peers = ring[1:] + near + far
    for peer in peers:
        pl.semaphore_signal(
            barrier, inc=1, device_id=peer, device_id_type=pl.DeviceIdType.MESH
        )
    pl.semaphore_wait(barrier, len(peers))

    order = [2, 1, 3] if n == 4 else list(range(1, n))
    x_out = [
        send(x_hbm, x_all.at[me], xsend.at[a - 1], xrecv.at[a - 1], ring[a])
        for a in range(1, n)
    ]
    g_out = [
        send(g_hbm, g_all.at[me], gsend.at[a - 1], grecv.at[a - 1], ring[a])
        for a in range(1, n)
    ]
    for a in order:
        x_out[a - 1].start()

    loads[2].wait()
    by_row = onehot_rows(rows, 32, pixels)
    by_col = onehot_cols(LANES, rows, pixels)
    same = lax.rem(iota((rows, rows), 0), pixels) == lax.rem(iota((rows, rows), 1), pixels)
    offs = 2 * frames - 1
    ahead = lax.rem(iota((offs, LANES), 1) + (frames - 1), LANES)
    spread = (iota((offs, LANES), 0) == ahead).astype(F32)
    wide = nn(bias[...], spread, lax.Precision.HIGHEST)
    for h in range(heads):
        line = jnp.broadcast_to(wide[h : h + 1, :], (32, LANES))
        table = pltpu.roll(line, 0, 1, stride=1, stride_axis=0)
        tall = nn(by_row, table, lax.Precision.HIGHEST)
        full = nn(tall, by_col, lax.Precision.HIGHEST)
        bm[h] = jnp.where(same, full, NEG)

    for load in loads[:2] + loads[3:]:
        load.wait()

    square = jnp.zeros((rows, 1), F32)
    for a in [0] + [n - b for b in order[1:] + order[:1]]:
        if a:
            x_out[n - a - 1].wait_recv()
        part = x_all[shard[a]].astype(F32)
        square = square + jnp.sum(part * part, axis=1, keepdims=True)
        xg[:, cols(a)] = (part * gain[:, cols(a)]).astype(BF16)
    for a in order:
        x_out[a - 1].wait_send()
    for a in order:
        g_out[a - 1].start()
    inv = lax.rsqrt(square * (1.0 / chans) + 1e-06)
    sinv[...] = jnp.broadcast_to(inv, (rows, LANES))

    head_of = lax.div(iota((rows, width), 1), head_dim)
    eye = (iota((width, width), 0) == iota((width, width), 1)).astype(BF16)

    qkv = nn(xg[...], w_all[...]) * inv
    q = (qkv[:, :width].astype(BF16).astype(F32) * scale).astype(BF16)
    k = qkv[:, width : 2 * width].astype(BF16)
    v = qkv[:, 2 * width :].astype(BF16)
    ks[...] = k
    vs[...] = v
    q_t[...] = nt(eye, q).astype(BF16)
    for h in range(heads):
        qm[h] = jnp.where(head_of == h, q.astype(F32), 0.0).astype(BF16)
        km[h] = jnp.where(head_of == h, k.astype(F32), 0.0).astype(BF16)
        vm[h] = jnp.where(head_of == h, v.astype(F32), 0.0).astype(BF16)

    att[...] = jnp.zeros((rows, width), F32)
    for h in range(heads):
        scores = nt(qm[h], ks[...]) + bm[h]
        top = jnp.max(scores, axis=1, keepdims=True)
        e = jnp.exp(scores - top)
        total = jnp.sum(e, axis=1, keepdims=True)
        p = (e * (1.0 / total)).astype(BF16)
        probs[h] = p
        att[...] += nn(p, vm[h])

    att_b = att[...].astype(BF16)
    m_out = [
        send(mix_send.at[a - 1], mix_recv.at[a - 1], msend.at[a - 1], mrecv.at[a - 1], ring[a])
        for a in range(1, n)
    ]
    for a in order:
        mix_send[a - 1] = nn(att_b, wo[:, cols(a)]).astype(BF16)
        m_out[a - 1].start()
    mix_own[...] = nn(att_b, wo[:, cols(0)])

    for a in range(1, n):
        g_out[a - 1].wait()
    ga_f = nt(g_all[0], wo[:, :width])
    for s in range(1, n):
        ga_f = ga_f + nt(g_all[s], wo[:, s * width : (s + 1) * width])
    ga = ga_f.astype(BF16)
    ga_t[...] = nt(eye, ga).astype(BF16)
    for h in range(heads):
        gam[h] = jnp.where(head_of == h, ga.astype(F32), 0.0).astype(BF16)

    last_first = (
        lax.div(iota((32, rows), 1), pixels) == (frames - 1) - iota((32, rows), 0)
    ).astype(BF16)
    gq_acc[...] = jnp.zeros((rows, width), F32)
    for h in range(heads):
        at = pl.ds(h * head_dim, head_dim)
        p = probs[h].astype(F32)
        grad_p = nt(gam[h], vs[...])
        dot = jnp.sum(p * grad_p, axis=1, keepdims=True)
        grad_s = (p * (grad_p - dot)).astype(BF16)
        gq_acc[...] += nn(grad_s, km[h])
        gk_t[at, :] = nn(q_t[at, :], grad_s).astype(BF16)
        gv_t[at, :] = nn(ga_t[at, :], probs[h]).astype(BF16)
        gsum[h] = nn(last_first, grad_s)

    eye_r = (iota((rows, rows), 0) == iota((rows, rows), 1)).astype(BF16)
    gq = (gq_acc[...] * scale).astype(BF16)
    gk_f = nt(eye_r, gk_t[...])
    gv_f = nt(eye_r, gv_t[...])
    gcat[:, :width] = gq
    gcat[:, width : 2 * width] = gk_f.astype(BF16)
    gcat[:, 2 * width :] = gv_f.astype(BF16)
    qf = functools.reduce(jnp.add, [qm[h] for h in range(heads)])
    dots = (
        gq.astype(F32) * qf.astype(F32) * (1.0 / scale)
        + gk_f * ks[...].astype(F32)
        + gv_f * vs[...].astype(F32)
    )
    inv = sinv[:, :1]
    mean = jnp.sum(dots, axis=1, keepdims=True) * (inv * inv * (1.0 / chans))

    i_out = [
        send(ig_send.at[a - 1], ig_recv.at[a - 1], isend.at[a - 1], irecv.at[a - 1], ring[a])
        for a in range(1, n)
    ]
    p_out = [
        send(p0_send.at[a - 1], p0_recv.at[a - 1], p0s.at[a - 1], p0r.at[a - 1], ring[a])
        for a in range(1, n)
    ]
    own_gain = None
    for a in order + [0]:
        back = nt(gcat[...], w_all[cols(a), :])
        part = x_all[shard[a]].astype(F32)
        gain_part = jnp.sum(back * (part * inv), axis=0, keepdims=True)
        share = back * (gain[:, cols(a)] * inv) - part * mean
        if a:
            p0_send[a - 1] = gain_part
            p_out[a - 1].start()
            ig_send[a - 1] = share.astype(BF16)
            i_out[a - 1].start()
        else:
            own_gain = gain_part
            ig_own[...] = share

    by_key = onehot_rows(rows, LANES, pixels)
    for h in range(heads):
        pairs = nn(gsum[h], by_key, lax.Precision.HIGHEST)
        moved = pltpu.roll(pairs, 0, 1, stride=1, stride_axis=0)
        pay1[:, width + LANES * h : width + LANES * (h + 1)] = jnp.sum(moved, axis=0, keepdims=True)

    for a in range(1, n):
        p_out[a - 1].wait()
        own_gain = own_gain + p0_recv[a - 1]
    pay1[:, :width] = own_gain
    n_out = [
        send(pay1, near_recv.at[j], nsend.at[j], nrecv.at[j], peer) for j, peer in enumerate(near)
    ]
    for copy in n_out:
        copy.start()

    for a in range(1, n):
        m_out[a - 1].wait()
    mixed = mix_own[...]
    for a in range(1, n):
        mixed = mixed + mix_recv[a - 1].astype(F32)
    bo_st[...] = (x_all[me].astype(F32) + mixed).astype(BF16)
    store_bo = pltpu.make_async_copy(bo_st, bo_hbm, lsem.at[8])
    store_bo.start()

    total = pay1[...]
    for j, copy in enumerate(n_out):
        copy.wait()
        total = total + near_recv[j]
    pay2[...] = total
    f_out = [
        send(pay2, far_recv.at[j], fsend.at[j], frecv.at[j], peer) for j, peer in enumerate(far)
    ]
    for copy in f_out:
        copy.start()

    for a in range(1, n):
        i_out[a - 1].wait()
    grad = ig_own[...] + g_all[me].astype(F32)
    for a in range(1, n):
        grad = grad + ig_recv[a - 1].astype(F32)
    ig_st[...] = grad.astype(BF16)
    store_ig = pltpu.make_async_copy(ig_st, ig_hbm, lsem.at[9])
    store_ig.start()

    total = pay2[...]
    for j, copy in enumerate(f_out):
        copy.wait()
        total = total + far_recv[j]
    gg_ref[...] = total[:, :width]
    for h in range(heads):
        bb_ref[h : h + 1, :] = total[:, width + LANES * h : width + LANES * h + offs]
    store_bo.wait()
    store_ig.wait()


def split_axis(size, parts):
    return (size // parts, parts) if size % parts == 0 else (size, 1)


def per_device(mesh_shape, inputs, out_grad, norm_gain, pos_bias, w_query, w_key, w_value, w_out):
    clips, frames, pixels, width = inputs.shape
    heads = pos_bias.shape[0]
    n = mesh_shape["tm"]
    chans = width * n
    rows = clips * frames * pixels
    xs, zl = split_axis(mesh_shape["dp"], 8)
    zh, cores = split_axis(mesh_shape["space"], 2)
    near, far = zl * cores - 1, xs * zh - 1
    pay = width + LANES * heads
    cfg = (frames, pixels, heads, n, xs, zl, zh, cores)
    vmem, dma = pltpu.VMEM, pltpu.SemaphoreType.DMA
    anywhere = pl.BlockSpec(memory_space=pl.ANY)
    in_vmem = pl.BlockSpec(memory_space=pltpu.VMEM)
    bo, ig, gg, bb = pl.pallas_call(
        functools.partial(kernel, cfg),
        out_shape=(
            jax.ShapeDtypeStruct((rows, width), BF16),
            jax.ShapeDtypeStruct((rows, width), BF16),
            jax.ShapeDtypeStruct((1, width), F32),
            jax.ShapeDtypeStruct(pos_bias.shape, F32),
        ),
        in_specs=[anywhere] * 8,
        out_specs=(anywhere, anywhere, in_vmem, in_vmem),
        scratch_shapes=[
            vmem((n, rows, width), BF16),
            vmem((n, rows, width), BF16),
            vmem((chans, 3 * width), BF16),
            vmem((width, chans), BF16),
            vmem((1, chans), F32),
            vmem(pos_bias.shape, F32),
            vmem((heads, rows, rows), F32),
            vmem((heads, rows, rows), BF16),
            vmem((rows, chans), BF16),
            vmem((heads, rows, width), BF16),
            vmem((heads, rows, width), BF16),
            vmem((heads, rows, width), BF16),
            vmem((heads, rows, width), BF16),
            vmem((rows, width), BF16),
            vmem((rows, width), BF16),
            vmem((width, rows), BF16),
            vmem((width, rows), BF16),
            vmem((rows, LANES), F32),
            vmem((rows, width), F32),
            vmem((rows, width), F32),
            vmem((width, rows), BF16),
            vmem((width, rows), BF16),
            vmem((rows, 3 * width), BF16),
            vmem((heads, 32, rows), F32),
            vmem((rows, width), F32),
            vmem((n - 1, rows, width), BF16),
            vmem((n - 1, rows, width), BF16),
            vmem((rows, width), F32),
            vmem((n - 1, rows, width), BF16),
            vmem((n - 1, rows, width), BF16),
            vmem((n - 1, 1, width), F32),
            vmem((n - 1, 1, width), F32),
            vmem((1, pay), F32),
            vmem((near, 1, pay), F32),
            vmem((1, pay), F32),
            vmem((far, 1, pay), F32),
            vmem((rows, width), BF16),
            vmem((rows, width), BF16),
            dma((10,)),
        ]
        + [dma((n - 1,))] * 10
        + [dma((near,)), dma((near,)), dma((far,)), dma((far,))],
        compiler_params=pltpu.CompilerParams(
            collective_id=0, has_side_effects=True, vmem_limit_bytes=56 * 1024 * 1024
        ),
    )(
        inputs.reshape(rows, width),
        out_grad.reshape(rows, width),
        norm_gain.reshape(1, chans),
        pos_bias,
        w_query,
        w_key,
        w_value,
        w_out,
    )
    return bo.reshape(inputs.shape), ig.reshape(inputs.shape), gg.reshape(width), bb


def solution(mesh):
    return jax.shard_map(
        functools.partial(per_device, dict(mesh.shape)),
        mesh=mesh,
        in_specs=(
            P("dp", None, "space", "tm"),
            P("dp", None, "space", "tm"),
            P(),
            P("tm", None),
            P(None, "tm"),
            P(None, "tm"),
            P(None, "tm"),
            P("tm", None),
        ),
        out_specs=(
            P("dp", None, "space", "tm"),
            P("dp", None, "space", "tm"),
            P("tm"),
            P("tm", None),
        ),
        check_vma=False,
    )
```

time: 1180 us -> 81 us (0.07)
  the two profiles are of different devices: /device:TPU:130 before, /device:TPU:1 now
where the time goes in v1:
time: 81 us; the launch traced here: 79.4 us
  Pallas kernels  75.2 us (93%)
  local copies, waits for them, and re-layouts  3.55 us (4%)
    pallas_call x1, Pallas kernels, per_device(): pl.pallas_call(functools.partial(kernel, cfg), out_shape=(jax.ShapeDtypeS...  75.2 us
    unnamed x10, local copies, waits for them, and re-layouts  3.55 us

profile of v1, /device:TPU:1, one launch (start us, length us, event | category | flops | bytes accessed | tf_op | source)
XLA Modules:
  0.0 79.4 jit_solution(8745681045818960768)
XLA Ops:
  0.6 75.2 %shard_map.111 = (bf16[320,256]{1,0:T(8,128)(2,1)}, bf16[320,256]{1,0:T(8,128)(2,1)}, f32[1,256]{1,0:T(1,128)}, f32[4,39]{1,0:T(4,128)}) custom-call(bf16[320,256]{1,0:T(8,128)(2,1)} %bitcast.8, bf16[320,256]{1,0:T(8,128)(2,1)} %bitcast.9, f32[1,1024]{1,0:T(1,128)} %bitcast.10, f32[4,39]{1,0:T(4,128)} %bias_hbm.1, bf16[1024,256]{1,0:T(8,128)(2,1)} %wq_hbm.1, ...), custom_call_target="tpu_custom_call" | custom-call | tf_op jit(solution)/shard_map/pallas_call | solution.py:386
  75.8 0.0 copy-start
  75.8 1.6 %copy.16 = bf16[1,20,16,256]{3,2,1,0:T(8,128)(2,1)} copy(bf16[1,20,16,256]{3,2,1,0:T(8,128)(2,1)} %bitcast.7) | data formatting | bytes 327680
  77.5 0.0 copy-done
  77.5 0.0 copy-start.2
  77.5 0.7 copy.17
  78.1 0.0 copy-done.2
  78.1 0.0 copy-start.1
  78.2 0.6 copy.18
  78.7 0.1 copy-done.1
  78.8 0.6 copy.19
Async XLA Ops:
  75.8 1.6 %copy-start = (bf16[320,256]{1,0:T(8,128)(2,1)S(1)}, bf16[320,256]{1,0:T(8,128)(2,1)}, u32[]{:S(2)}) copy-start(bf16[320,256]{1,0:T(8,128)(2,1)} %get-tuple-element.9) | copy-start | bytes 491524
  77.5 0.7 copy-start.2
  78.1 0.7 copy-start.1

commit v2 on v1

--- a/solution.py
+++ b/solution.py
@@ -77,15 +77,27 @@
     gcat,
     gsum,
     mix_own,
-    mix_send,
-    mix_recv,
+    mix_opp,
+    mix_dir,
+    mix_part,
+    mix_sum,
+    mix_ropp,
+    mix_rdir,
+    mix_rsum,
     ig_own,
-    ig_send,
-    ig_recv,
-    p0_send,
-    p0_recv,
+    ig_opp,
+    ig_dir,
+    ig_part,
+    ig_sum,
+    ig_ropp,
+    ig_rdir,
+    ig_rsum,
+    slices,
+    slices_recv,
+    pay0,
+    pay0_recv,
     pay1,
-    near_recv,
+    mid_recv,
     pay2,
     far_recv,
     bo_st,
@@ -99,37 +111,56 @@
     mrecv,
     isend,
     irecv,
-    p0s,
-    p0r,
+    ssend,
+    srecv,
+    csend,
+    crecv,
     nsend,
     nrecv,
     fsend,
     frecv,
 ):
-    frames, pixels, heads, n, xs, zl, zh, cores = cfg
+    frames, pixels, heads, n, xs, za_lo, za_hi, zb, cores = cfg
     rows, width = x_hbm.shape
     chans = width * n
     head_dim = width // heads
     scale = head_dim ** (-0.5)
+    half = rows // 2
+    lo, hi = pl.ds(0, half), pl.ds(half, half)
     me = lax.axis_index("tm")
     dp = lax.axis_index("dp")
     sp = lax.axis_index("space")
-    my_x, my_zl = lax.div(dp, zl), lax.rem(dp, zl)
-    my_zh, my_core = lax.div(sp, cores), lax.rem(sp, cores)
-
-    ring = [(dp, sp, lax.rem(me + a, n)) for a in range(n)]
+    my_core = lax.rem(sp, cores)
+    run = lax.rem(dp, za_lo * zb)
+    my_x, my_zb = lax.div(dp, za_lo * zb), lax.rem(run, zb)
+    my_za = lax.div(sp, cores) * za_lo + lax.div(run, zb)
+
+    def device(x, a, b, core, y):
+        return (
+            (x * za_lo + lax.rem(a, za_lo)) * zb + b,
+            lax.div(a, za_lo) * cores + core,
+            y,
+        )
+
     shard = [lax.rem(me + a, n) for a in range(n)]
-    near = [
-        (my_x * zl + lax.rem(my_zl + b, zl), my_zh * cores + lax.rem(my_core + d, cores), me)
-        for b in range(zl)
-        for d in range(cores)
+    ring = [(dp, sp, shard[a]) for a in range(n)]
+    slice_to = [
+        (a, device(my_x, my_za, my_zb, lax.rem(my_core + c, cores), shard[a]))
+        for a in (2, 1, 3)
+        for c in range(cores)
+    ]
+    twins = [
+        device(my_x, my_za, my_zb, lax.rem(my_core + c, cores), me) for c in range(1, cores)
+    ]
+    mid = [
+        device(lax.rem(my_x + b, xs), my_za, lax.rem(my_zb + d, zb), my_core, me)
+        for b in range(xs)
+        for d in range(zb)
         if b or d
     ]
     far = [
-        (lax.rem(my_x + b, xs) * zl + my_zl, lax.rem(my_zh + d, zh) * cores + my_core, me)
-        for b in range(xs)
-        for d in range(zh)
-        if b or d
+        device(my_x, lax.rem(my_za + a, za_lo * za_hi), my_zb, my_core, me)
+        for a in range(1, za_lo * za_hi)
     ]
 
     def send(src, dst, ssem, rsem, to):
@@ -142,13 +173,39 @@
             device_id_type=pl.DeviceIdType.MESH,
         )
 
+    def gather(src, dst, ssem, rsem):
+        moves = [
+            (src.at[lo], dst.at[me, lo], 1),
+            (src.at[hi], dst.at[me, hi], 3),
+            (src.at[hi], dst.at[me, hi], 1),
+            (src.at[lo], dst.at[me, lo], 3),
+            (dst.at[shard[3], lo], dst.at[shard[3], lo], 1),
+            (dst.at[shard[1], hi], dst.at[shard[1], hi], 3),
+        ]
+        return [
+            send(s, d, ssem.at[i], rsem.at[i], ring[a]) for i, (s, d, a) in enumerate(moves)
+        ]
+
+    def scatter(opp, direct, total, ropp, rdir, rsum, ssem, rsem):
+        moves = [
+            (opp.at[lo], ropp.at[0], 1),
+            (opp.at[hi], ropp.at[1], 3),
+            (direct.at[0], rdir.at[0], 3),
+            (direct.at[1], rdir.at[1], 1),
+            (total.at[0], rsum.at[0], 1),
+            (total.at[1], rsum.at[1], 3),
+        ]
+        return [
+            send(s, d, ssem.at[i], rsem.at[i], ring[a]) for i, (s, d, a) in enumerate(moves)
+        ]
+
     def cols(a):
         return pl.ds(pl.multiple_of(shard[a] * width, width), width)
 
     loads = [
+        pltpu.make_async_copy(bias_hbm, bias, lsem.at[2]),
         pltpu.make_async_copy(x_hbm, x_all.at[me], lsem.at[0]),
         pltpu.make_async_copy(gain_hbm, gain, lsem.at[1]),
-        pltpu.make_async_copy(bias_hbm, bias, lsem.at[2]),
         pltpu.make_async_copy(wq_hbm, w_all.at[:, pl.ds(0, width)], lsem.at[3]),
         pltpu.make_async_copy(wk_hbm, w_all.at[:, pl.ds(width, width)], lsem.at[4]),
         pltpu.make_async_copy(wv_hbm, w_all.at[:, pl.ds(2 * width, width)], lsem.at[5]),
@@ -159,26 +216,13 @@
         load.start()
 
     barrier = pltpu.get_barrier_semaphore()
-    peers = ring[1:] + near + far
+    peers = [to for _, to in slice_to] + twins + mid + far
     for peer in peers:
         pl.semaphore_signal(
             barrier, inc=1, device_id=peer, device_id_type=pl.DeviceIdType.MESH
         )
-    pl.semaphore_wait(barrier, len(peers))
-
-    order = [2, 1, 3] if n == 4 else list(range(1, n))
-    x_out = [
-        send(x_hbm, x_all.at[me], xsend.at[a - 1], xrecv.at[a - 1], ring[a])
-        for a in range(1, n)
-    ]
-    g_out = [
-        send(g_hbm, g_all.at[me], gsend.at[a - 1], grecv.at[a - 1], ring[a])
-        for a in range(1, n)
-    ]
-    for a in order:
-        x_out[a - 1].start()
-
-    loads[2].wait()
+
+    loads[0].wait()
     by_row = onehot_rows(rows, 32, pixels)
     by_col = onehot_cols(LANES, rows, pixels)
     same = lax.rem(iota((rows, rows), 0), pixels) == lax.rem(iota((rows, rows), 1), pixels)
@@ -193,20 +237,34 @@
         full = nn(tall, by_col, lax.Precision.HIGHEST)
         bm[h] = jnp.where(same, full, NEG)
 
-    for load in loads[:2] + loads[3:]:
+    pl.semaphore_wait(barrier, len(peers))
+
+    x_out = gather(x_hbm, x_all, xsend, xrecv)
+    g_out = gather(g_hbm, g_all, gsend, grecv)
+    for copy in x_out[:4]:
+        copy.start()
+    for load in loads[1:]:
         load.wait()
 
-    square = jnp.zeros((rows, 1), F32)
-    for a in [0] + [n - b for b in order[1:] + order[:1]]:
-        if a:
-            x_out[n - a - 1].wait_recv()
+    def take(a, square):
         part = x_all[shard[a]].astype(F32)
-        square = square + jnp.sum(part * part, axis=1, keepdims=True)
         xg[:, cols(a)] = (part * gain[:, cols(a)]).astype(BF16)
-    for a in order:
-        x_out[a - 1].wait_send()
-    for a in order:
-        g_out[a - 1].start()
+        return square + jnp.sum(part * part, axis=1, keepdims=True)
+
+    square = take(0, jnp.zeros((rows, 1), F32))
+    x_out[0].wait_recv()
+    x_out[4].start()
+    x_out[1].wait_recv()
+    x_out[5].start()
+    for copy in g_out[:4]:
+        copy.start()
+    x_out[2].wait_recv()
+    square = take(3, square)
+    x_out[3].wait_recv()
+    square = take(1, square)
+    x_out[4].wait_recv()
+    x_out[5].wait_recv()
+    square = take(2, square)
     inv = lax.rsqrt(square * (1.0 / chans) + 1e-06)
     sinv[...] = jnp.broadcast_to(inv, (rows, LANES))
 
@@ -234,22 +292,35 @@
         p = (e * (1.0 / total)).astype(BF16)
         probs[h] = p
         att[...] += nn(p, vm[h])
+        if h == 0:
+            g_out[0].wait_recv()
+            g_out[4].start()
+            g_out[1].wait_recv()
+            g_out[5].start()
 
     att_b = att[...].astype(BF16)
-    m_out = [
-        send(mix_send.at[a - 1], mix_recv.at[a - 1], msend.at[a - 1], mrecv.at[a - 1], ring[a])
-        for a in range(1, n)
-    ]
-    for a in order:
-        mix_send[a - 1] = nn(att_b, wo[:, cols(a)]).astype(BF16)
-        m_out[a - 1].start()
+    m_out = scatter(mix_opp, mix_dir, mix_sum, mix_ropp, mix_rdir, mix_rsum, msend, mrecv)
+    mix_opp[...] = nn(att_b, wo[:, cols(2)]).astype(BF16)
+    m_out[0].start()
+    m_out[1].start()
+    part = nn(att_b, wo[:, cols(3)])
+    mix_dir[0] = part[:half].astype(BF16)
+    mix_part[1] = part[half:]
+    m_out[2].start()
+    part = nn(att_b, wo[:, cols(1)])
+    mix_part[0] = part[:half]
+    mix_dir[1] = part[half:].astype(BF16)
+    m_out[3].start()
     mix_own[...] = nn(att_b, wo[:, cols(0)])
 
-    for a in range(1, n):
-        g_out[a - 1].wait()
-    ga_f = nt(g_all[0], wo[:, :width])
-    for s in range(1, n):
-        ga_f = ga_f + nt(g_all[s], wo[:, s * width : (s + 1) * width])
+    ga_f = nt(g_all[me], wo[:, cols(0)])
+    g_out[2].wait_recv()
+    ga_f = ga_f + nt(g_all[shard[3]], wo[:, cols(3)])
+    g_out[3].wait_recv()
+    ga_f = ga_f + nt(g_all[shard[1]], wo[:, cols(1)])
+    g_out[4].wait_recv()
+    g_out[5].wait_recv()
+    ga_f = ga_f + nt(g_all[shard[2]], wo[:, cols(2)])
     ga = ga_f.astype(BF16)
     ga_t[...] = nt(eye, ga).astype(BF16)
     for h in range(heads):
@@ -286,58 +357,87 @@
     inv = sinv[:, :1]
     mean = jnp.sum(dots, axis=1, keepdims=True) * (inv * inv * (1.0 / chans))
 
-    i_out = [
-        send(ig_send.at[a - 1], ig_recv.at[a - 1], isend.at[a - 1], irecv.at[a - 1], ring[a])
-        for a in range(1, n)
-    ]
-    p_out = [
-        send(p0_send.at[a - 1], p0_recv.at[a - 1], p0s.at[a - 1], p0r.at[a - 1], ring[a])
-        for a in range(1, n)
+    s_out = [
+        send(slices.at[a - 1], slices_recv.at[j], ssend.at[j], srecv.at[j], to)
+        for j, (a, to) in enumerate(slice_to)
     ]
     own_gain = None
-    for a in order + [0]:
+    i_out = scatter(ig_opp, ig_dir, ig_sum, ig_ropp, ig_rdir, ig_rsum, isend, irecv)
+    for a in (2, 1, 3, 0):
         back = nt(gcat[...], w_all[cols(a), :])
         part = x_all[shard[a]].astype(F32)
         gain_part = jnp.sum(back * (part * inv), axis=0, keepdims=True)
         share = back * (gain[:, cols(a)] * inv) - part * mean
         if a:
-            p0_send[a - 1] = gain_part
-            p_out[a - 1].start()
-            ig_send[a - 1] = share.astype(BF16)
-            i_out[a - 1].start()
-        else:
+            slices[a - 1] = gain_part
+            for j, (b, _) in enumerate(slice_to):
+                if a == b:
+                    s_out[j].start()
+        if a == 0:
             own_gain = gain_part
             ig_own[...] = share
+        elif a == 2:
+            ig_opp[...] = share.astype(BF16)
+        elif a == 1:
+            ig_part[0] = share[:half]
+            ig_dir[1] = share[half:].astype(BF16)
+        else:
+            ig_dir[0] = share[:half].astype(BF16)
+            ig_part[1] = share[half:]
 
     by_key = onehot_rows(rows, LANES, pixels)
-    for h in range(heads):
-        pairs = nn(gsum[h], by_key, lax.Precision.HIGHEST)
-        moved = pltpu.roll(pairs, 0, 1, stride=1, stride_axis=0)
-        pay1[:, width + LANES * h : width + LANES * (h + 1)] = jnp.sum(moved, axis=0, keepdims=True)
-
-    for a in range(1, n):
-        p_out[a - 1].wait()
-        own_gain = own_gain + p0_recv[a - 1]
-    pay1[:, :width] = own_gain
+    for h in range(0, heads, 2):
+        pair = jnp.zeros((1, LANES), F32)
+        for side in range(2):
+            pairs = nn(gsum[h + side], by_key, lax.Precision.HIGHEST)
+            moved = pltpu.roll(pairs, 0, 1, stride=1, stride_axis=0)
+            line = jnp.sum(moved, axis=0, keepdims=True)
+            pair = pair + (pltpu.roll(line, LANES // 2, 1) if side else line)
+        pay0[:, width + LANES // 2 * h : width + LANES // 2 * (h + 2)] = pair
+    pay0[:, :width] = own_gain
+    c_out = [
+        send(pay0, pay0_recv.at[j], csend.at[j], crecv.at[j], to) for j, to in enumerate(twins)
+    ]
+    for copy in c_out:
+        copy.start()
+
+    def add_opposite(out, part, ropp, total):
+        for side in range(2):
+            out[side].wait_recv()
+            total[side] = (part[side] + ropp[side].astype(F32)).astype(BF16)
+            out[4 + side].start()
+
+    add_opposite(m_out, mix_part, mix_ropp, mix_sum)
+    for copy in i_out[:4]:
+        copy.start()
+
+    total = pay0[...]
+    for j, copy in enumerate(c_out):
+        copy.wait_recv()
+        total = total + pay0_recv[j]
+    pay1[...] = total
+    for j, copy in enumerate(s_out):
+        copy.wait_recv()
+        pay1[:, :width] += slices_recv[j]
     n_out = [
-        send(pay1, near_recv.at[j], nsend.at[j], nrecv.at[j], peer) for j, peer in enumerate(near)
+        send(pay1, mid_recv.at[j], nsend.at[j], nrecv.at[j], peer) for j, peer in enumerate(mid)
     ]
     for copy in n_out:
         copy.start()
 
-    for a in range(1, n):
-        m_out[a - 1].wait()
-    mixed = mix_own[...]
-    for a in range(1, n):
-        mixed = mixed + mix_recv[a - 1].astype(F32)
-    bo_st[...] = (x_all[me].astype(F32) + mixed).astype(BF16)
-    store_bo = pltpu.make_async_copy(bo_st, bo_hbm, lsem.at[8])
-    store_bo.start()
-
+    def finish(first, own, out, rdir, rsum, staged):
+        for copy in out[2:]:
+            copy.wait_recv()
+        for side in range(2):
+            at = pl.ds(side * half, half)
+            got = rdir[side].astype(F32) + rsum[side].astype(F32)
+            staged[at, :] = (first[me, at].astype(F32) + own[at, :] + got).astype(BF16)
+
+    add_opposite(i_out, ig_part, ig_ropp, ig_sum)
     total = pay1[...]
     for j, copy in enumerate(n_out):
-        copy.wait()
-        total = total + near_recv[j]
+        copy.wait_recv()
+        total = total + mid_recv[j]
     pay2[...] = total
     f_out = [
         send(pay2, far_recv.at[j], fsend.at[j], frecv.at[j], peer) for j, peer in enumerate(far)
@@ -345,28 +445,39 @@
     for copy in f_out:
         copy.start()
 
-    for a in range(1, n):
-        i_out[a - 1].wait()
-    grad = ig_own[...] + g_all[me].astype(F32)
-    for a in range(1, n):
-        grad = grad + ig_recv[a - 1].astype(F32)
-    ig_st[...] = grad.astype(BF16)
+    finish(x_all, mix_own, m_out, mix_rdir, mix_rsum, bo_st)
+    store_bo = pltpu.make_async_copy(bo_st, bo_hbm, lsem.at[8])
+    store_bo.start()
+    finish(g_all, ig_own, i_out, ig_rdir, ig_rsum, ig_st)
     store_ig = pltpu.make_async_copy(ig_st, ig_hbm, lsem.at[9])
     store_ig.start()
+    for copy in x_out + g_out + m_out + i_out + s_out + c_out + n_out:
+        copy.wait_send()
+    store_bo.wait()
+    store_ig.wait()
 
     total = pay2[...]
     for j, copy in enumerate(f_out):
-        copy.wait()
+        copy.wait_recv()
         total = total + far_recv[j]
     gg_ref[...] = total[:, :width]
     for h in range(heads):
-        bb_ref[h : h + 1, :] = total[:, width + LANES * h : width + LANES * h + offs]
-    store_bo.wait()
-    store_ig.wait()
-
-
-def split_axis(size, parts):
-    return (size // parts, parts) if size % parts == 0 else (size, 1)
+        first = width + LANES // 2 * h
+        bb_ref[h : h + 1, :] = total[:, first : first + offs]
+    for copy in f_out:
+        copy.wait_send()
+
+
+def hand_over(*refs):
+    count = (len(refs) - 1) // 2
+    copies = [
+        pltpu.make_async_copy(src, dst, refs[-1].at[i])
+        for i, (src, dst) in enumerate(zip(refs[:count], refs[count:-1]))
+    ]
+    for copy in copies:
+        copy.start()
+    for copy in copies:
+        copy.wait()
 
 
 def per_device(mesh_shape, inputs, out_grad, norm_gain, pos_bias, w_query, w_key, w_value, w_out):
@@ -375,22 +486,31 @@
     n = mesh_shape["tm"]
     chans = width * n
     rows = clips * frames * pixels
-    xs, zl = split_axis(mesh_shape["dp"], 8)
-    zh, cores = split_axis(mesh_shape["space"], 2)
-    near, far = zl * cores - 1, xs * zh - 1
-    pay = width + LANES * heads
-    cfg = (frames, pixels, heads, n, xs, zl, zh, cores)
+    half = rows // 2
+    cores, zb = 2, 4 if mesh_shape["dp"] % 8 == 0 else 1
+    za_lo = 2 if mesh_shape["dp"] % 8 == 0 else 1
+    xs, za_hi = mesh_shape["dp"] // (za_lo * zb), mesh_shape["space"] // cores
+    mid, far = max(1, xs * zb - 1), max(1, za_lo * za_hi - 1)
+    pay = width + LANES // 2 * heads
+    cfg = (frames, pixels, heads, n, xs, za_lo, za_hi, zb, cores)
     vmem, dma = pltpu.VMEM, pltpu.SemaphoreType.DMA
     anywhere = pl.BlockSpec(memory_space=pl.ANY)
     in_vmem = pl.BlockSpec(memory_space=pltpu.VMEM)
-    bo, ig, gg, bb = pl.pallas_call(
+    sums = [
+        vmem((rows, width), F32),
+        vmem((rows, width), BF16),
+        vmem((2, half, width), BF16),
+        vmem((2, half, width), F32),
+    ] + [vmem((2, half, width), BF16)] * 4
+    results = (
+        jax.ShapeDtypeStruct((rows, width), BF16),
+        jax.ShapeDtypeStruct((rows, width), BF16),
+        jax.ShapeDtypeStruct((1, width), F32),
+        jax.ShapeDtypeStruct(pos_bias.shape, F32),
+    )
+    made = pl.pallas_call(
         functools.partial(kernel, cfg),
-        out_shape=(
-            jax.ShapeDtypeStruct((rows, width), BF16),
-            jax.ShapeDtypeStruct((rows, width), BF16),
-            jax.ShapeDtypeStruct((1, width), F32),
-            jax.ShapeDtypeStruct(pos_bias.shape, F32),
-        ),
+        out_shape=results,
         in_specs=[anywhere] * 8,
         out_specs=(anywhere, anywhere, in_vmem, in_vmem),
         scratch_shapes=[
@@ -418,24 +538,27 @@
             vmem((width, rows), BF16),
             vmem((rows, 3 * width), BF16),
             vmem((heads, 32, rows), F32),
-            vmem((rows, width), F32),
-            vmem((n - 1, rows, width), BF16),
-            vmem((n - 1, rows, width), BF16),
-            vmem((rows, width), F32),
-            vmem((n - 1, rows, width), BF16),
-            vmem((n - 1, rows, width), BF16),
+        ]
+        + sums
+        + sums
+        + [
             vmem((n - 1, 1, width), F32),
-            vmem((n - 1, 1, width), F32),
+            vmem(((n - 1) * cores, 1, width), F32),
             vmem((1, pay), F32),
-            vmem((near, 1, pay), F32),
+            vmem((cores - 1, 1, pay), F32),
+            vmem((1, pay), F32),
+            vmem((mid, 1, pay), F32),
             vmem((1, pay), F32),
             vmem((far, 1, pay), F32),
             vmem((rows, width), BF16),
             vmem((rows, width), BF16),
             dma((10,)),
         ]
-        + [dma((n - 1,))] * 10
-        + [dma((near,)), dma((near,)), dma((far,)), dma((far,))],
+        + [dma((6,))] * 8
+        + [dma(((n - 1) * cores,))] * 2
+        + [dma((cores - 1,))] * 2
+        + [dma((mid,))] * 2
+        + [dma((far,))] * 2,
         compiler_params=pltpu.CompilerParams(
             collective_id=0, has_side_effects=True, vmem_limit_bytes=56 * 1024 * 1024
         ),
@@ -449,6 +572,13 @@
         w_value,
         w_out,
     )
+    bo, ig, gg, bb = pl.pallas_call(
+        hand_over,
+        out_shape=results,
+        in_specs=[anywhere] * 4,
+        out_specs=(anywhere,) * 4,
+        scratch_shapes=[dma((4,))],
+    )(*made)
     return bo.reshape(inputs.shape), ig.reshape(inputs.shape), gg.reshape(width), bb
 
 

time: 81 us -> 78 us (0.963); the launches traced: 79.4 us -> 77.8 us
  local copies, waits for them, and re-layouts: 3.55 us -> 0 us
  Pallas kernels: 75.2 us -> 77.2 us
    unnamed x10 -> x0, local copies, waits for them, and re-layouts: 3.55 us -> none
    pallas_call x1 -> x2, Pallas kernels: 75.2 us -> 77.2 us  [the longest x1 66 us: per_device(): pl.pallas_call(functools.partial(kernel, cfg), out_shape=results, in_spec...]
where the time goes in v2:
time: 78 us; the launch traced here: 77.8 us
  Pallas kernels  77.2 us (99%)
    pallas_call x1, Pallas kernels, per_device(): pl.pallas_call(functools.partial(kernel, cfg), out_shape=results, in_spec...  66 us
    pallas_call x1, Pallas kernels, per_device(): pl.pallas_call(hand_over, out_shape=results, in_specs=[anywhere] * 4, out...  11.2 us

profile of v2, /device:TPU:1, one launch (start us, length us, event | category | flops | bytes accessed | tf_op | source)
XLA Modules:
  0.0 77.8 jit_solution(8240408657637419289)
XLA Ops:
  0.6 66.0 %shard_map.111 = (bf16[320,256]{1,0:T(8,128)(2,1)}, bf16[320,256]{1,0:T(8,128)(2,1)}, f32[1,256]{1,0:T(1,128)}, f32[4,39]{1,0:T(4,128)}) custom-call(bf16[320,256]{1,0:T(8,128)(2,1)} %bitcast.6, bf16[320,256]{1,0:T(8,128)(2,1)} %bitcast.7, f32[1,1024]{1,0:T(1,128)} %bitcast.8, f32[4,39]{1,0:T(4,128)} %bias_hbm.1, bf16[1024,256]{1,0:T(8,128)(2,1)} %wq_hbm.1, ...), custom_call_target="tpu_custom_call" | custom-call | tf_op jit(solution)/shard_map/pallas_call | solution.py:511
  66.6 11.2 %shard_map.112 = (bf16[320,256]{1,0:T(8,128)(2,1)}, bf16[320,256]{1,0:T(8,128)(2,1)}, f32[1,256]{1,0:T(1,128)}, f32[4,39]{1,0:T(4,128)}) custom-call(bf16[320,256]{1,0:T(8,128)(2,1)} %get-tuple-element.12.refs_0_, bf16[320,256]{1,0:T(8,128)(2,1)} %get-tuple-element.13.refs_1_, f32[1,256]{1,0:T(1,128)} %get-tuple-element.14.refs_2_, ...), custom_call_target="tpu_custom_call" | custom-call | tf_op jit(solution)/shard_map/pallas_call | solution.py:575

commit v3 on v2

--- a/solution.py
+++ b/solution.py
@@ -48,8 +48,8 @@
     wk_hbm,
     wv_hbm,
     wo_hbm,
-    bo_hbm,
-    ig_hbm,
+    bo_ref,
+    ig_ref,
     gg_ref,
     bb_ref,
     x_all,
@@ -100,8 +100,7 @@
     mid_recv,
     pay2,
     far_recv,
-    bo_st,
-    ig_st,
+    back,
     lsem,
     xsend,
     xrecv,
@@ -223,19 +222,25 @@
         )
 
     loads[0].wait()
-    by_row = onehot_rows(rows, 32, pixels)
-    by_col = onehot_cols(LANES, rows, pixels)
+    by_row = onehot_rows(rows, 32, pixels).astype(BF16)
+    by_col = onehot_cols(LANES, rows, pixels).astype(BF16)
+    by_col = jnp.concatenate([by_col, by_col], axis=0)
     same = lax.rem(iota((rows, rows), 0), pixels) == lax.rem(iota((rows, rows), 1), pixels)
     offs = 2 * frames - 1
     ahead = lax.rem(iota((offs, LANES), 1) + (frames - 1), LANES)
     spread = (iota((offs, LANES), 0) == ahead).astype(F32)
     wide = nn(bias[...], spread, lax.Precision.HIGHEST)
-    for h in range(heads):
+
+    def bias_table(h):
         line = jnp.broadcast_to(wide[h : h + 1, :], (32, LANES))
         table = pltpu.roll(line, 0, 1, stride=1, stride_axis=0)
-        tall = nn(by_row, table, lax.Precision.HIGHEST)
-        full = nn(tall, by_col, lax.Precision.HIGHEST)
-        bm[h] = jnp.where(same, full, NEG)
+        high = table.astype(BF16)
+        low = (table - high.astype(F32)).astype(BF16)
+        tall = nn(by_row, jnp.concatenate([high, low], axis=1)).astype(BF16)
+        bm[h] = jnp.where(same, nn(tall, by_col), NEG)
+
+    for h in range(heads // 2):
+        bias_table(h)
 
     pl.semaphore_wait(barrier, len(peers))
 
@@ -243,6 +248,8 @@
     g_out = gather(g_hbm, g_all, gsend, grecv)
     for copy in x_out[:4]:
         copy.start()
+    for h in range(heads // 2, heads):
+        bias_table(h)
     for load in loads[1:]:
         load.wait()
 
@@ -348,43 +355,22 @@
     gcat[:, :width] = gq
     gcat[:, width : 2 * width] = gk_f.astype(BF16)
     gcat[:, 2 * width :] = gv_f.astype(BF16)
-    qf = functools.reduce(jnp.add, [qm[h] for h in range(heads)])
-    dots = (
-        gq.astype(F32) * qf.astype(F32) * (1.0 / scale)
-        + gk_f * ks[...].astype(F32)
-        + gv_f * vs[...].astype(F32)
-    )
     inv = sinv[:, :1]
-    mean = jnp.sum(dots, axis=1, keepdims=True) * (inv * inv * (1.0 / chans))
 
     s_out = [
         send(slices.at[a - 1], slices_recv.at[j], ssend.at[j], srecv.at[j], to)
         for j, (a, to) in enumerate(slice_to)
     ]
-    own_gain = None
-    i_out = scatter(ig_opp, ig_dir, ig_sum, ig_ropp, ig_rdir, ig_rsum, isend, irecv)
     for a in (2, 1, 3, 0):
-        back = nt(gcat[...], w_all[cols(a), :])
-        part = x_all[shard[a]].astype(F32)
-        gain_part = jnp.sum(back * (part * inv), axis=0, keepdims=True)
-        share = back * (gain[:, cols(a)] * inv) - part * mean
+        back[a] = nt(gcat[...], w_all[cols(a), :])
+        gain_part = jnp.sum(back[a] * (x_all[shard[a]].astype(F32) * inv), axis=0, keepdims=True)
         if a:
             slices[a - 1] = gain_part
             for j, (b, _) in enumerate(slice_to):
                 if a == b:
                     s_out[j].start()
-        if a == 0:
-            own_gain = gain_part
-            ig_own[...] = share
-        elif a == 2:
-            ig_opp[...] = share.astype(BF16)
-        elif a == 1:
-            ig_part[0] = share[:half]
-            ig_dir[1] = share[half:].astype(BF16)
         else:
-            ig_dir[0] = share[:half].astype(BF16)
-            ig_part[1] = share[half:]
-
+            pay0[:, :width] = gain_part
     by_key = onehot_rows(rows, LANES, pixels)
     for h in range(0, heads, 2):
         pair = jnp.zeros((1, LANES), F32)
@@ -394,7 +380,6 @@
             line = jnp.sum(moved, axis=0, keepdims=True)
             pair = pair + (pltpu.roll(line, LANES // 2, 1) if side else line)
         pay0[:, width + LANES // 2 * h : width + LANES // 2 * (h + 2)] = pair
-    pay0[:, :width] = own_gain
     c_out = [
         send(pay0, pay0_recv.at[j], csend.at[j], crecv.at[j], to) for j, to in enumerate(twins)
     ]
@@ -408,8 +393,23 @@
             out[4 + side].start()
 
     add_opposite(m_out, mix_part, mix_ropp, mix_sum)
-    for copy in i_out[:4]:
-        copy.start()
+
+    qf = functools.reduce(jnp.add, [qm[h] for h in range(heads)])
+    dots = (
+        gq.astype(F32) * qf.astype(F32) * (1.0 / scale)
+        + gk_f * ks[...].astype(F32)
+        + gv_f * vs[...].astype(F32)
+    )
+    mean = jnp.sum(dots, axis=1, keepdims=True) * (inv * inv * (1.0 / chans))
+    i_out = scatter(ig_opp, ig_dir, ig_sum, ig_ropp, ig_rdir, ig_rsum, isend, irecv)
+
+    def share(a):
+        part = x_all[shard[a]].astype(F32)
+        return back[a] * (gain[:, cols(a)] * inv) - part * mean
+
+    ig_opp[...] = share(2).astype(BF16)
+    i_out[0].start()
+    i_out[1].start()
 
     total = pay0[...]
     for j, copy in enumerate(c_out):
@@ -425,6 +425,16 @@
     for copy in n_out:
         copy.start()
 
+    part = share(3)
+    ig_dir[0] = part[:half].astype(BF16)
+    ig_part[1] = part[half:]
+    i_out[2].start()
+    part = share(1)
+    ig_part[0] = part[:half]
+    ig_dir[1] = part[half:].astype(BF16)
+    i_out[3].start()
+    ig_own[...] = share(0)
+
     def finish(first, own, out, rdir, rsum, staged):
         for copy in out[2:]:
             copy.wait_recv()
@@ -445,16 +455,10 @@
     for copy in f_out:
         copy.start()
 
-    finish(x_all, mix_own, m_out, mix_rdir, mix_rsum, bo_st)
-    store_bo = pltpu.make_async_copy(bo_st, bo_hbm, lsem.at[8])
-    store_bo.start()
-    finish(g_all, ig_own, i_out, ig_rdir, ig_rsum, ig_st)
-    store_ig = pltpu.make_async_copy(ig_st, ig_hbm, lsem.at[9])
-    store_ig.start()
+    finish(x_all, mix_own, m_out, mix_rdir, mix_rsum, bo_ref)
+    finish(g_all, ig_own, i_out, ig_rdir, ig_rsum, ig_ref)
     for copy in x_out + g_out + m_out + i_out + s_out + c_out + n_out:
         copy.wait_send()
-    store_bo.wait()
-    store_ig.wait()
 
     total = pay2[...]
     for j, copy in enumerate(f_out):
@@ -510,9 +514,9 @@
     )
     made = pl.pallas_call(
         functools.partial(kernel, cfg),
-        out_shape=results,
+        out_shape=tuple(vmem(r.shape, r.dtype) for r in results),
         in_specs=[anywhere] * 8,
-        out_specs=(anywhere, anywhere, in_vmem, in_vmem),
+        out_specs=(in_vmem,) * 4,
         scratch_shapes=[
             vmem((n, rows, width), BF16),
             vmem((n, rows, width), BF16),
@@ -550,9 +554,8 @@
             vmem((mid, 1, pay), F32),
             vmem((1, pay), F32),
             vmem((far, 1, pay), F32),
-            vmem((rows, width), BF16),
-            vmem((rows, width), BF16),
-            dma((10,)),
+            vmem((n, rows, width), F32),
+            dma((8,)),
         ]
         + [dma((6,))] * 8
         + [dma(((n - 1) * cores,))] * 2
@@ -575,10 +578,10 @@
     bo, ig, gg, bb = pl.pallas_call(
         hand_over,
         out_shape=results,
-        in_specs=[anywhere] * 4,
+        in_specs=[in_vmem] * 4,
         out_specs=(anywhere,) * 4,
         scratch_shapes=[dma((4,))],
-    )(*made)
+    )(*[pltpu.with_memory_space_constraint(m, pltpu.VMEM) for m in made])
     return bo.reshape(inputs.shape), ig.reshape(inputs.shape), gg.reshape(width), bb
 
 

time: 78 us -> 66.9 us (0.86)
  Pallas kernels: 77.2 us -> 66.1 us
    pallas_call x2, Pallas kernels: 77.2 us -> 66.1 us  [the longest x1 65.3 us: per_device(): pl.pallas_call(functools.partial(kernel, cfg), out_shape=tuple((vmem(r.sh...]
where the time goes in v3:
time: 66.9 us; the launch traced here: 66.7 us
  Pallas kernels  66.1 us (99%)
    pallas_call x1, Pallas kernels, per_device(): pl.pallas_call(functools.partial(kernel, cfg), out_shape=tuple((vmem(r.sh...  65.3 us

profile of v3, /device:TPU:1, one launch (start us, length us, event | category | flops | bytes accessed | tf_op | source)
XLA Modules:
  0.0 66.7 jit_solution(16695429028338469279)
XLA Ops:
  0.6 65.3 %shard_map.111 = (bf16[320,256]{1,0:T(8,128)(2,1)S(1)}, bf16[320,256]{1,0:T(8,128)(2,1)S(1)}, f32[1,256]{1,0:T(1,128)S(1)}, f32[4,39]{1,0:T(4,128)S(1)}) custom-call(bf16[320,256]{1,0:T(8,128)(2,1)} %bitcast.6, bf16[320,256]{1,0:T(8,128)(2,1)} %bitcast.7, f32[1,1024]{1,0:T(1,128)} %bitcast.8, f32[4,39]{1,0:T(4,128)} %bias_hbm.1, bf16[1024,256]{1,0:T(8,128)(2,1)} %wq_hbm.1, ...), custom_call_target="tpu_custom_call" | custom-call | tf_op jit(solution)/shard_map/pallas_call | solution.py:515
  66.0 0.8 %shard_map.112 = (bf16[320,256]{1,0:T(8,128)(2,1)}, bf16[320,256]{1,0:T(8,128)(2,1)}, f32[1,256]{1,0:T(1,128)}, f32[4,39]{1,0:T(4,128)}) custom-call(bf16[320,256]{1,0:T(8,128)(2,1)S(1)} %get-tuple-element.12.refs_0_, bf16[320,256]{1,0:T(8,128)(2,1)S(1)} %get-tuple-element.13.refs_1_, f32[1,256]{1,0:T(1,128)S(1)} %get-tuple-element.14.refs_2_, ...), custom_call_target="tpu_custom_call" | custom-call | tf_op jit(solution)/shard_map/pallas_call | solution.py:578

commit v4 on v3

--- a/solution.py
+++ b/solution.py
@@ -101,6 +101,7 @@
     pay2,
     far_recv,
     back,
+    scaled,
     lsem,
     xsend,
     xrecv,
@@ -173,17 +174,27 @@
         )
 
     def gather(src, dst, ssem, rsem):
+        piece = [pl.ds(i * (rows // 4), rows // 4) for i in range(4)]
         moves = [
-            (src.at[lo], dst.at[me, lo], 1),
-            (src.at[hi], dst.at[me, hi], 3),
+            (src.at[piece[0]], dst.at[me, piece[0]], 1),
+            (src.at[piece[2]], dst.at[me, piece[2]], 3),
+            (src.at[piece[1]], dst.at[me, piece[1]], 1),
+            (src.at[piece[3]], dst.at[me, piece[3]], 3),
             (src.at[hi], dst.at[me, hi], 1),
             (src.at[lo], dst.at[me, lo], 3),
-            (dst.at[shard[3], lo], dst.at[shard[3], lo], 1),
-            (dst.at[shard[1], hi], dst.at[shard[1], hi], 3),
+            (dst.at[shard[3], piece[0]], dst.at[shard[3], piece[0]], 1),
+            (dst.at[shard[1], piece[2]], dst.at[shard[1], piece[2]], 3),
+            (dst.at[shard[3], piece[1]], dst.at[shard[3], piece[1]], 1),
+            (dst.at[shard[1], piece[3]], dst.at[shard[1], piece[3]], 3),
         ]
         return [
             send(s, d, ssem.at[i], rsem.at[i], ring[a]) for i, (s, d, a) in enumerate(moves)
         ]
+
+    def pass_on(out, which):
+        for i in which:
+            out[i].wait_recv()
+            out[6 + i].start()
 
     def scatter(opp, direct, total, ropp, rdir, rsum, ssem, rsem):
         moves = [
@@ -201,25 +212,25 @@
     def cols(a):
         return pl.ds(pl.multiple_of(shard[a] * width, width), width)
 
+    barrier = pltpu.get_barrier_semaphore()
+    peers = mid + [to for _, to in slice_to] + twins + far
+    for peer in peers:
+        pl.semaphore_signal(
+            barrier, inc=1, device_id=peer, device_id_type=pl.DeviceIdType.MESH
+        )
+
     loads = [
         pltpu.make_async_copy(bias_hbm, bias, lsem.at[2]),
         pltpu.make_async_copy(x_hbm, x_all.at[me], lsem.at[0]),
         pltpu.make_async_copy(gain_hbm, gain, lsem.at[1]),
-        pltpu.make_async_copy(wq_hbm, w_all.at[:, pl.ds(0, width)], lsem.at[3]),
-        pltpu.make_async_copy(wk_hbm, w_all.at[:, pl.ds(width, width)], lsem.at[4]),
-        pltpu.make_async_copy(wv_hbm, w_all.at[:, pl.ds(2 * width, width)], lsem.at[5]),
+        pltpu.make_async_copy(wq_hbm, w_all.at[0], lsem.at[3]),
+        pltpu.make_async_copy(wk_hbm, w_all.at[1], lsem.at[4]),
+        pltpu.make_async_copy(wv_hbm, w_all.at[2], lsem.at[5]),
         pltpu.make_async_copy(wo_hbm, wo, lsem.at[6]),
         pltpu.make_async_copy(g_hbm, g_all.at[me], lsem.at[7]),
     ]
     for load in loads:
         load.start()
-
-    barrier = pltpu.get_barrier_semaphore()
-    peers = [to for _, to in slice_to] + twins + mid + far
-    for peer in peers:
-        pl.semaphore_signal(
-            barrier, inc=1, device_id=peer, device_id_type=pl.DeviceIdType.MESH
-        )
 
     loads[0].wait()
     by_row = onehot_rows(rows, 32, pixels).astype(BF16)
@@ -246,64 +257,63 @@
 
     x_out = gather(x_hbm, x_all, xsend, xrecv)
     g_out = gather(g_hbm, g_all, gsend, grecv)
-    for copy in x_out[:4]:
+    for copy in x_out[:6]:
         copy.start()
     for h in range(heads // 2, heads):
         bias_table(h)
-    for load in loads[1:]:
-        load.wait()
-
     def take(a, square):
         part = x_all[shard[a]].astype(F32)
         xg[:, cols(a)] = (part * gain[:, cols(a)]).astype(BF16)
         return square + jnp.sum(part * part, axis=1, keepdims=True)
 
+    pass_on(x_out, range(4))
+    for copy in g_out[:6]:
+        copy.start()
+    for load in loads[1:]:
+        load.wait()
     square = take(0, jnp.zeros((rows, 1), F32))
-    x_out[0].wait_recv()
-    x_out[4].start()
-    x_out[1].wait_recv()
-    x_out[5].start()
-    for copy in g_out[:4]:
-        copy.start()
-    x_out[2].wait_recv()
+    x_out[4].wait_recv()
     square = take(3, square)
-    x_out[3].wait_recv()
+    x_out[5].wait_recv()
     square = take(1, square)
-    x_out[4].wait_recv()
-    x_out[5].wait_recv()
+    for copy in x_out[6:]:
+        copy.wait_recv()
     square = take(2, square)
     inv = lax.rsqrt(square * (1.0 / chans) + 1e-06)
     sinv[...] = jnp.broadcast_to(inv, (rows, LANES))
 
-    head_of = lax.div(iota((rows, width), 1), head_dim)
+    head_of = lax.div(iota((rows, LANES), 1), head_dim)
+    pair = [slice(h // 2 * LANES, h // 2 * LANES + LANES) for h in range(heads)]
+
+    def alone(a, h):
+        return jnp.where(head_of == h % 2, a[:, pair[h]].astype(F32), 0.0).astype(BF16)
+
     eye = (iota((width, width), 0) == iota((width, width), 1)).astype(BF16)
 
-    qkv = nn(xg[...], w_all[...]) * inv
-    q = (qkv[:, :width].astype(BF16).astype(F32) * scale).astype(BF16)
-    k = qkv[:, width : 2 * width].astype(BF16)
-    v = qkv[:, 2 * width :].astype(BF16)
+    q = ((nn(xg[...], w_all[0]) * inv).astype(BF16).astype(F32) * scale).astype(BF16)
+    k = (nn(xg[...], w_all[1]) * inv).astype(BF16)
+    v = (nn(xg[...], w_all[2]) * inv).astype(BF16)
     ks[...] = k
     vs[...] = v
     q_t[...] = nt(eye, q).astype(BF16)
     for h in range(heads):
-        qm[h] = jnp.where(head_of == h, q.astype(F32), 0.0).astype(BF16)
-        km[h] = jnp.where(head_of == h, k.astype(F32), 0.0).astype(BF16)
-        vm[h] = jnp.where(head_of == h, v.astype(F32), 0.0).astype(BF16)
-
-    att[...] = jnp.zeros((rows, width), F32)
+        qm[h] = alone(q, h)
+        km[h] = alone(k, h)
+        vm[h] = alone(v, h)
+
     for h in range(heads):
-        scores = nt(qm[h], ks[...]) + bm[h]
+        scores = nt(qm[h], ks[:, pair[h]]) + bm[h]
         top = jnp.max(scores, axis=1, keepdims=True)
         e = jnp.exp(scores - top)
         total = jnp.sum(e, axis=1, keepdims=True)
         p = (e * (1.0 / total)).astype(BF16)
         probs[h] = p
-        att[...] += nn(p, vm[h])
-        if h == 0:
-            g_out[0].wait_recv()
-            g_out[4].start()
-            g_out[1].wait_recv()
-            g_out[5].start()
+        if h % 2:
+            att[:, pair[h]] += nn(p, vm[h])
+        else:
+            att[:, pair[h]] = nn(p, vm[h])
+        if h < 2:
+            pass_on(g_out, (2 * h, 2 * h + 1))
 
     att_b = att[...].astype(BF16)
     m_out = scatter(mix_opp, mix_dir, mix_sum, mix_ropp, mix_rdir, mix_rsum, msend, mrecv)
@@ -320,30 +330,36 @@
     m_out[3].start()
     mix_own[...] = nn(att_b, wo[:, cols(0)])
 
+    inv = sinv[:, :1]
+    for a in range(n):
+        scaled[a] = x_all[shard[a]].astype(F32) * inv
+
     ga_f = nt(g_all[me], wo[:, cols(0)])
-    g_out[2].wait_recv()
+    g_out[4].wait_recv()
     ga_f = ga_f + nt(g_all[shard[3]], wo[:, cols(3)])
-    g_out[3].wait_recv()
+    g_out[5].wait_recv()
     ga_f = ga_f + nt(g_all[shard[1]], wo[:, cols(1)])
-    g_out[4].wait_recv()
-    g_out[5].wait_recv()
+    for copy in g_out[6:]:
+        copy.wait_recv()
     ga_f = ga_f + nt(g_all[shard[2]], wo[:, cols(2)])
     ga = ga_f.astype(BF16)
     ga_t[...] = nt(eye, ga).astype(BF16)
     for h in range(heads):
-        gam[h] = jnp.where(head_of == h, ga.astype(F32), 0.0).astype(BF16)
+        gam[h] = alone(ga, h)
 
     last_first = (
         lax.div(iota((32, rows), 1), pixels) == (frames - 1) - iota((32, rows), 0)
     ).astype(BF16)
-    gq_acc[...] = jnp.zeros((rows, width), F32)
     for h in range(heads):
         at = pl.ds(h * head_dim, head_dim)
         p = probs[h].astype(F32)
-        grad_p = nt(gam[h], vs[...])
-        dot = jnp.sum(p * grad_p, axis=1, keepdims=True)
+        grad_p = nt(gam[h], vs[:, pair[h]])
+        dot = jnp.sum(gam[h].astype(F32) * att[:, pair[h]], axis=1, keepdims=True)
         grad_s = (p * (grad_p - dot)).astype(BF16)
-        gq_acc[...] += nn(grad_s, km[h])
+        if h % 2:
+            gq_acc[:, pair[h]] += nn(grad_s, km[h])
+        else:
+            gq_acc[:, pair[h]] = nn(grad_s, km[h])
         gk_t[at, :] = nn(q_t[at, :], grad_s).astype(BF16)
         gv_t[at, :] = nn(ga_t[at, :], probs[h]).astype(BF16)
         gsum[h] = nn(last_first, grad_s)
@@ -355,15 +371,17 @@
     gcat[:, :width] = gq
     gcat[:, width : 2 * width] = gk_f.astype(BF16)
     gcat[:, 2 * width :] = gv_f.astype(BF16)
-    inv = sinv[:, :1]
-
     s_out = [
         send(slices.at[a - 1], slices_recv.at[j], ssend.at[j], srecv.at[j], to)
         for j, (a, to) in enumerate(slice_to)
     ]
     for a in (2, 1, 3, 0):
-        back[a] = nt(gcat[...], w_all[cols(a), :])
-        gain_part = jnp.sum(back[a] * (x_all[shard[a]].astype(F32) * inv), axis=0, keepdims=True)
+        back[a] = (
+            nt(gcat[:, :width], w_all[0, cols(a), :])
+            + nt(gcat[:, width : 2 * width], w_all[1, cols(a), :])
+            + nt(gcat[:, 2 * width :], w_all[2, cols(a), :])
+        )
+        gain_part = jnp.sum(back[a] * scaled[a], axis=0, keepdims=True)
         if a:
             slices[a - 1] = gain_part
             for j, (b, _) in enumerate(slice_to):
@@ -373,13 +391,13 @@
             pay0[:, :width] = gain_part
     by_key = onehot_rows(rows, LANES, pixels)
     for h in range(0, heads, 2):
-        pair = jnp.zeros((1, LANES), F32)
+        both = jnp.zeros((1, LANES), F32)
         for side in range(2):
             pairs = nn(gsum[h + side], by_key, lax.Precision.HIGHEST)
             moved = pltpu.roll(pairs, 0, 1, stride=1, stride_axis=0)
             line = jnp.sum(moved, axis=0, keepdims=True)
-            pair = pair + (pltpu.roll(line, LANES // 2, 1) if side else line)
-        pay0[:, width + LANES // 2 * h : width + LANES // 2 * (h + 2)] = pair
+            both = both + (pltpu.roll(line, LANES // 2, 1) if side else line)
+        pay0[:, width + LANES // 2 * h : width + LANES // 2 * (h + 2)] = both
     c_out = [
         send(pay0, pay0_recv.at[j], csend.at[j], crecv.at[j], to) for j, to in enumerate(twins)
     ]
@@ -394,7 +412,7 @@
 
     add_opposite(m_out, mix_part, mix_ropp, mix_sum)
 
-    qf = functools.reduce(jnp.add, [qm[h] for h in range(heads)])
+    qf = jnp.concatenate([qm[h] + qm[h + 1] for h in range(0, heads, 2)], axis=1)
     dots = (
         gq.astype(F32) * qf.astype(F32) * (1.0 / scale)
         + gk_f * ks[...].astype(F32)
@@ -443,7 +461,6 @@
             got = rdir[side].astype(F32) + rsum[side].astype(F32)
             staged[at, :] = (first[me, at].astype(F32) + own[at, :] + got).astype(BF16)
 
-    add_opposite(i_out, ig_part, ig_ropp, ig_sum)
     total = pay1[...]
     for j, copy in enumerate(n_out):
         copy.wait_recv()
@@ -455,6 +472,7 @@
     for copy in f_out:
         copy.start()
 
+    add_opposite(i_out, ig_part, ig_ropp, ig_sum)
     finish(x_all, mix_own, m_out, mix_rdir, mix_rsum, bo_ref)
     finish(g_all, ig_own, i_out, ig_rdir, ig_rsum, ig_ref)
     for copy in x_out + g_out + m_out + i_out + s_out + c_out + n_out:
@@ -520,17 +538,17 @@
         scratch_shapes=[
             vmem((n, rows, width), BF16),
             vmem((n, rows, width), BF16),
-            vmem((chans, 3 * width), BF16),
+            vmem((3, chans, width), BF16),
             vmem((width, chans), BF16),
             vmem((1, chans), F32),
             vmem(pos_bias.shape, F32),
             vmem((heads, rows, rows), F32),
             vmem((heads, rows, rows), BF16),
             vmem((rows, chans), BF16),
-            vmem((heads, rows, width), BF16),
-            vmem((heads, rows, width), BF16),
-            vmem((heads, rows, width), BF16),
-            vmem((heads, rows, width), BF16),
+            vmem((heads, rows, LANES), BF16),
+            vmem((heads, rows, LANES), BF16),
+            vmem((heads, rows, LANES), BF16),
+            vmem((heads, rows, LANES), BF16),
             vmem((rows, width), BF16),
             vmem((rows, width), BF16),
             vmem((width, rows), BF16),
@@ -555,9 +573,11 @@
             vmem((1, pay), F32),
             vmem((far, 1, pay), F32),
             vmem((n, rows, width), F32),
+            vmem((n, rows, width), F32),
             dma((8,)),
         ]
-        + [dma((6,))] * 8
+        + [dma((10,))] * 4
+        + [dma((6,))] * 4
         + [dma(((n - 1) * cores,))] * 2
         + [dma((cores - 1,))] * 2
         + [dma((mid,))] * 2

time: 66.9 us -> 66.5 us (level)
  no operation moved by 1% of the time
where the time goes in v4:
time: 66.5 us; the launch traced here: 66.4 us
  Pallas kernels  65.7 us (99%)
    pallas_call x1, Pallas kernels, per_device(): pl.pallas_call(functools.partial(kernel, cfg), out_shape=tuple((vmem(r.sh...  65 us

profile of v4, /device:TPU:1, one launch (start us, length us, event | category | flops | bytes accessed | tf_op | source)
XLA Modules:
  0.0 66.4 jit_solution(14575595242362767946)
XLA Ops:
  0.6 65.0 %shard_map.111 = (bf16[320,256]{1,0:T(8,128)(2,1)S(1)}, bf16[320,256]{1,0:T(8,128)(2,1)S(1)}, f32[1,256]{1,0:T(1,128)S(1)}, f32[4,39]{1,0:T(4,128)S(1)}) custom-call(bf16[320,256]{1,0:T(8,128)(2,1)} %bitcast.6, bf16[320,256]{1,0:T(8,128)(2,1)} %bitcast.7, f32[1,1024]{1,0:T(1,128)} %bitcast.8, f32[4,39]{1,0:T(4,128)} %bias_hbm.1, bf16[1024,256]{1,0:T(8,128)(2,1)} %wq_hbm.1, ...), custom_call_target="tpu_custom_call" | custom-call | tf_op jit(solution)/shard_map/pallas_call | solution.py:533
  65.6 0.8 %shard_map.112 = (bf16[320,256]{1,0:T(8,128)(2,1)}, bf16[320,256]{1,0:T(8,128)(2,1)}, f32[1,256]{1,0:T(1,128)}, f32[4,39]{1,0:T(4,128)}) custom-call(bf16[320,256]{1,0:T(8,128)(2,1)S(1)} %get-tuple-element.12.refs_0_, bf16[320,256]{1,0:T(8,128)(2,1)S(1)} %get-tuple-element.13.refs_1_, f32[1,256]{1,0:T(1,128)S(1)} %get-tuple-element.14.refs_2_, ...), custom_call_target="tpu_custom_call" | custom-call | tf_op jit(solution)/shard_map/pallas_call | solution.py:598

commit v5 on v4

--- a/solution.py
+++ b/solution.py
@@ -213,7 +213,7 @@
         return pl.ds(pl.multiple_of(shard[a] * width, width), width)
 
     barrier = pltpu.get_barrier_semaphore()
-    peers = mid + [to for _, to in slice_to] + twins + far
+    peers = far + mid + [to for _, to in slice_to] + twins
     for peer in peers:
         pl.semaphore_signal(
             barrier, inc=1, device_id=peer, device_id_type=pl.DeviceIdType.MESH
@@ -328,7 +328,6 @@
     mix_part[0] = part[:half]
     mix_dir[1] = part[half:].astype(BF16)
     m_out[3].start()
-    mix_own[...] = nn(att_b, wo[:, cols(0)])
 
     inv = sinv[:, :1]
     for a in range(n):
@@ -410,6 +409,7 @@
             total[side] = (part[side] + ropp[side].astype(F32)).astype(BF16)
             out[4 + side].start()
 
+    mix_own[...] = nn(att[...].astype(BF16), wo[:, cols(0)])
     add_opposite(m_out, mix_part, mix_ropp, mix_sum)
 
     qf = jnp.concatenate([qm[h] + qm[h + 1] for h in range(0, heads, 2)], axis=1)

time: 66.5 us -> 66.3 us (level)
  no operation moved by 1% of the time
where the time goes in v5:
time: 66.3 us; the launch traced here: 66.2 us
  Pallas kernels  65.5 us (99%)
    pallas_call x1, Pallas kernels, per_device(): pl.pallas_call(functools.partial(kernel, cfg), out_shape=tuple((vmem(r.sh...  64.8 us

profile of v5, /device:TPU:1, one launch (start us, length us, event | category | flops | bytes accessed | tf_op | source)
XLA Modules:
  0.0 66.2 jit_solution(3859385044853705827)
XLA Ops:
  0.6 64.8 %shard_map.111 = (bf16[320,256]{1,0:T(8,128)(2,1)S(1)}, bf16[320,256]{1,0:T(8,128)(2,1)S(1)}, f32[1,256]{1,0:T(1,128)S(1)}, f32[4,39]{1,0:T(4,128)S(1)}) custom-call(bf16[320,256]{1,0:T(8,128)(2,1)} %bitcast.6, bf16[320,256]{1,0:T(8,128)(2,1)} %bitcast.7, f32[1,1024]{1,0:T(1,128)} %bitcast.8, f32[4,39]{1,0:T(4,128)} %bias_hbm.1, bf16[1024,256]{1,0:T(8,128)(2,1)} %wq_hbm.1, ...), custom_call_target="tpu_custom_call" | custom-call | tf_op jit(solution)/shard_map/pallas_call | solution.py:533
  65.4 0.8 %shard_map.112 = (bf16[320,256]{1,0:T(8,128)(2,1)}, bf16[320,256]{1,0:T(8,128)(2,1)}, f32[1,256]{1,0:T(1,128)}, f32[4,39]{1,0:T(4,128)}) custom-call(bf16[320,256]{1,0:T(8,128)(2,1)S(1)} %get-tuple-element.12.refs_0_, bf16[320,256]{1,0:T(8,128)(2,1)S(1)} %get-tuple-element.13.refs_1_, f32[1,256]{1,0:T(1,128)S(1)} %get-tuple-element.14.refs_2_, ...), custom_call_target="tpu_custom_call" | custom-call | tf_op jit(solution)/shard_map/pallas_call | solution.py:598
